TPU v7x, 256 devices: a whole 4x4x8 slice. The times are simulated.
256 devices in a mesh: tile: 32 (over z, x_hi, core), group: 8 (over y, x_lo).
Axes of the slice: x: 4 (x_hi: 2, x_lo: 2; x = x_hi * 2 + x_lo), y: 4, z: 8, core: 2. Of those that a mesh axis runs over, the one named last changes fastest.
Arguments:
- object_field: float32 [2, 320, 4096], P(None, 'group', 'tile'), may hold values from -6 to 6
- probe_field: float32 [2, 256, 256], replicated, may hold values from -6 to 6
- amplitudes: float32 [256, 256, 256], P(('tile', 'group')), may hold values from 0 to 4
- row_start: int32 [256], P(('tile', 'group')), may hold values from 0 to 64
- column_start: int32 [256], P(('tile', 'group')), may hold values from 0 to 128
- live_slots: int32 [256], P(('tile', 'group')), may hold values 0 or 1
Outputs:
- new_object: float32 [2, 320, 4096], P(None, 'group', 'tile')
- new_probe: float32 [2, 256, 256], replicated
All inputs are finite; a program needn't handle non-finite values. No bound on the sum of `live_slots` on one device may be relied on, other than what follows from the above.
Results may differ from a plain program's by a relative error of at most 0.0001.
Values sent between devices are 32-bit elements; how exact they have to be, the bound alone decides.
No kernel may reach another device: no remote copies, remote signals or barrier semaphores. Data moves between devices by JAX's collectives and lax.ppermute only.
A program may use at most 64 MiB of HBM per device.

v0:
```python
import math
import jax
import jax.numpy as jnp
from jax import lax
from jax.sharding import PartitionSpec as P

WIN = 256
HALO = 128


def padded_2(value, sides, width):
    for axis, dim in sides:
        count, length = (lax.axis_size(axis), value.shape[dim])
        up = [(i, (i + 1) % count) for i in range(count - 1)]
        down = [(j, i) for i, j in up]
        last = lax.slice_in_dim(value, length - width, length, axis=dim)
        initial = lax.slice_in_dim(value, 0, width, axis=dim)
        before = lax.ppermute(last, axis, up)
        after = lax.ppermute(initial, axis, down)
        value = jnp.concatenate([before, value, after], axis=dim)
    return value


def dft_tables(length):
    counter = jnp.arange(length, dtype=jnp.int32)
    product = counter[:, None] * counter[None, :] % length
    angles = 2.0 * math.pi / length * product.astype(jnp.float32)
    factor = 1.0 / math.sqrt(length)
    return (jnp.cos(angles) * factor, jnp.sin(angles) * factor)


def apply_left(matrix, values):
    return jnp.einsum("jk,pkl->pjl", matrix, values, precision=lax.Precision.HIGHEST)


def apply_right(values, matrix):
    return jnp.einsum("pjk,kl->pjl", values, matrix, precision=lax.Precision.HIGHEST)


def transform(real_part, imag_part, cos_table, sin_table, sign):
    left_real = apply_left(cos_table, real_part) - sign * apply_left(sin_table, imag_part)
    left_imag = apply_left(cos_table, imag_part) + sign * apply_left(sin_table, real_part)
    right_real = apply_right(left_real, cos_table) - sign * apply_right(left_imag, sin_table)
    right_imag = apply_right(left_imag, cos_table) + sign * apply_right(left_real, sin_table)
    return (right_real, right_imag)


def window_terms(windows, probe_field, amplitudes, live_slots, cos_table, sin_table):
    sample_real = windows[:, 0]
    sample_imag = windows[:, 1]
    probe_real = probe_field[0]
    probe_imag = probe_field[1]
    exit_real = probe_real * sample_real - probe_imag * sample_imag
    exit_imag = probe_real * sample_imag + probe_imag * sample_real
    far_real, far_imag = transform(exit_real, exit_imag, cos_table, sin_table, -1.0)
    modulus = jnp.maximum(jnp.sqrt(far_real * far_real + far_imag * far_imag), 0.25)
    factor = 1.0 - amplitudes / modulus
    miss_real, miss_imag = transform(
        far_real * factor, far_imag * factor, cos_table, sin_table, 1.0
    )
    weight = live_slots.astype(jnp.float32)[:, None, None]
    miss_real = miss_real * weight
    miss_imag = miss_imag * weight
    grad_real = probe_real * miss_real + probe_imag * miss_imag
    grad_imag = probe_real * miss_imag - probe_imag * miss_real
    probe_light = weight * (probe_real * probe_real + probe_imag * probe_imag)
    terms = jnp.stack([grad_real, grad_imag, probe_light], axis=1)
    probe_grad = jnp.stack(
        [
            jnp.sum(sample_real * miss_real + sample_imag * miss_imag, axis=0),
            jnp.sum(sample_real * miss_imag - sample_imag * miss_real, axis=0),
        ],
        axis=0,
    )
    window_light = jnp.sum(weight * (sample_real * sample_real + sample_imag * sample_imag), axis=0)
    return (terms, probe_grad, window_light)


def add_windows(accum, terms, top_rows, left_edges):
    zero_index = jnp.zeros((), jnp.int32)
    channels = terms.shape[1]

    def place(slot, current):
        corner = (zero_index, top_rows[slot], left_edges[slot])
        piece = lax.dynamic_slice(current, corner, (channels, WIN, WIN))
        return lax.dynamic_update_slice(current, piece + terms[slot], corner)

    return lax.fori_loop(0, terms.shape[0], place, accum)


def cut_windows(padded, top_rows, left_edges):
    zero_index = jnp.zeros((), jnp.int32)

    def single(top_row, left_edge):
        return lax.dynamic_slice(padded, (zero_index, top_row, left_edge), (2, WIN, WIN))

    return jax.vmap(single)(top_rows, left_edges)


def edge_strips(accum):
    return jnp.concatenate([accum[:, :, :HALO], accum[:, :, accum.shape[2] - HALO :]], axis=2)


def add_edges(inner, arrived):
    width = inner.shape[2]
    inner = inner.at[:, :, :HALO].add(arrived[:, :, :HALO])
    return inner.at[:, :, width - HALO :].add(arrived[:, :, arrived.shape[2] - HALO :])


def apply_updates(object_field, probe_field, share, probe_grad, window_light):
    light_max = jnp.max(probe_field[0] * probe_field[0] + probe_field[1] * probe_field[1]) + 1e-06
    new_object = object_field - share[0:2] / (share[2:3] + 0.25 * light_max)
    new_probe = (
        probe_field - probe_grad / (window_light + 0.25 * jnp.mean(window_light) + 1e-05)[None]
    )
    return (new_object, new_probe)


def local(object_field, probe_field, amplitudes, row_start, column_start, live_slots):
    cos_table, sin_table = dft_tables(WIN)
    full_rows = lax.all_gather(object_field, "group", axis=1, tiled=True)
    padded = padded_2(full_rows, (("tile", 2),), HALO)
    windows = cut_windows(padded, row_start, column_start)
    terms, probe_grad, window_light = window_terms(
        windows, probe_field, amplitudes, live_slots, cos_table, sin_table
    )
    accum = jnp.zeros((terms.shape[1], padded.shape[1], padded.shape[2]), jnp.float32)
    accum = add_windows(accum, terms, row_start, column_start)
    arrived = padded_2(edge_strips(accum), (("tile", 2),), HALO)
    summed = add_edges(accum[:, :, HALO : accum.shape[2] - HALO], arrived)
    share = lax.psum_scatter(summed, "group", scatter_dimension=1, tiled=True)
    probe_grad, window_light = lax.psum((probe_grad, window_light), ("tile", "group"))
    object_field, probe_field = apply_updates(
        object_field, probe_field, share, probe_grad, window_light
    )
    return (object_field, probe_field)


def solution(mesh):
    return jax.shard_map(
        local,
        mesh=mesh,
        in_specs=(
            P(None, "group", "tile"),
            P(),
            P(("tile", "group"), None, None),
            P(("tile", "group")),
            P(("tile", "group")),
            P(("tile", "group")),
        ),
        out_specs=(P(None, "group", "tile"), P()),
        check_vma=False,
    )
```

profile of v0, /device:TPU:2, one launch (start us, length us, event | category | flops | bytes accessed | tf_op | source)
XLA Modules:
  0.0 370.7 jit_solution(3378128131235949026)
XLA Ops:
  8.1 29.8 %all_gather.3 = f32[2,320,128]{2,1,0:T(8,128)S(1)} all-gather(f32[2,40,128]{2,1,0:T(8,128)} %param.14), channel_id=1, replica_groups=mesh['tile'=32,'group'=8] {'group'}, dimensions={1}, use_global_device_ids=true | all-gather | bytes 368640 | tf_op jit(solution)/shard_map/all_gather | solution.py:121
  39.2 3.1 collective-permute-start
  44.7 1.5 fusion.38
  46.2 1.5 fusion.34
  47.7 1.5 fusion.9
  49.2 1.5 fusion.7
  50.7 1.5 fusion.47
  52.2 1.5 fusion.48
  53.6 1.5 fusion.4
  55.1 1.7 bitcast_multiply_fusion.11
  58.4 1.5 fusion.27
  59.8 1.5 fusion.3
  61.3 1.5 fusion.2
  62.8 1.5 fusion.45
  64.3 1.5 fusion.46
  65.8 1.5 fusion
  67.3 1.7 fusion.1
  69.9 10.9 %dynamic_update_slice.4 = f32[3,320,384]{2,1,0:T(8,128)S(1)} dynamic-update-slice(f32[3,320,384]{2,1,0:T(8,128)S(1)} %broadcast_in_dim.6, f32[3,256,256]{2,1,0:T(8,128)S(1)} %maximum_bitcast_fusion, s32[]{:T(128)} %constant.112.clone.1, s32[]{:T(128)S(6)} %select_n.60, s32[]{:T(128)S(6)} %select_n.61) | dynamic-update-slice | bytes 1572868 | tf_op jit(solution)/shard_map/while/body/eval_jaxpr/dynamic_update_slice | solution.py:86
  81.6 6.6 %collective-permute-start.2 = (f32[3,320,128]{2,1,0:T(8,128)}, f32[3,320,128]{2,1,0:T(8,128)S(1)}, u32[]{:S(2)}, u32[]{:S(2)}) collective-permute-start(f32[3,320,128]{2,1,0:T(8,128)} %get-tuple-element.73), channel_id=1, source_target_pairs={{0,8},{8,16},{16,24},{24,32},{32,40},{40,48},{48,56},{56,64},{64,7... | collective-permute-start | bytes 1474568 | tf_op jit(solution)/shard_map/ppermute | solution.py:18
  91.3 4.5 %collective-permute-done.3 = f32[3,320,128]{2,1,0:T(8,128)} collective-permute-done((f32[3,320,128]{2,1,0:T(8,128)S(1)}, f32[3,320,128]{2,1,0:T(8,128)}, u32[]{:S(2)}, u32[]{:S(2)}) %collective-permute-start.3) | collective-permute-done | bytes 491552 | tf_op jit(solution)/shard_map/ppermute | solution.py:19
  95.7 1.9 fusion.13
  98.3 257.6 %all-reduce.3.cloned.1.call-done = (f32[2,256,256]{2,1,0:T(8,128)}, f32[256,256]{1,0:T(8,128)}) async-done(((f32[2,256,256]{2,1,0:T(8,128)}, f32[256,256]{1,0:T(8,128)}), (f32[2,256,256]{2,1,0:T(8,128)}, f32[256,256]{1,0:T(8,128)})) %all-reduce.3.cloned.1.call-update) | async-done | bytes 786448 | tf_op jit(solution)/shard_map/psum | solution.py:132
  355.9 1.6 reduce_sum.8
  359.2 1.9 divide_subtract_fusion
  (36 shorter events, 11.2 us)
Async XLA Ops:
  8.0 36.6 %copy-start = (f32[2,256,256]{2,1,0:T(8,128)S(1)}, f32[2,256,256]{2,1,0:T(8,128)}, u32[]{:S(2)}) copy-start(f32[2,256,256]{2,1,0:T(8,128)} %param.15) | copy-start | bytes 1572868
  8.0 347.9 %all-reduce.3.cloned.1.call-start = ((), (), s32[]{:S(2)}) async-start(), calls=%async_computation.2 | async-start | bytes 1572864 | tf_op jit(solution)/shard_map/psum | solution.py:132
  37.9 6.3 %collective-permute-start.1 = (f32[2,320,128]{2,1,0:T(8,128)S(1)}, f32[2,320,128]{2,1,0:T(8,128)S(1)}, u32[]{:S(2)}, u32[]{:S(2)}) collective-permute-start(f32[2,320,128]{2,1,0:T(8,128)S(1)} %all_gather.3), channel_id=1, source_target_pairs={{8,0},{16,8},{24,16},{32,24},{40,32},{48,40},{56,48},{64,56},{72,6... | collective-permute-start | bytes 983048 | tf_op jit(solution)/shard_map/ppermute | solution.py:19
  39.2 5.0 %collective-permute-start = (f32[2,320,128]{2,1,0:T(8,128)S(1)}, f32[2,320,128]{2,1,0:T(8,128)S(1)}, u32[]{:S(2)}, u32[]{:S(2)}) collective-permute-start(f32[2,320,128]{2,1,0:T(8,128)S(1)} %all_gather.3), channel_id=1, source_target_pairs={{0,8},{8,16},{16,24},{24,32},{32,40},{40,48},{48,56},{56,64},{64,7... | collective-permute-start | bytes 983048 | tf_op jit(solution)/shard_map/ppermute | solution.py:18
  52.1 3.0 copy-start.6
  67.3 2.4 copy-start.1
  69.0 0.8 copy-start.3
  80.8 8.8 %copy-start.2 = (f32[256,256]{1,0:T(8,128)S(1)}, f32[256,256]{1,0:T(8,128)}, u32[]{:S(2)}) copy-start(f32[256,256]{1,0:T(8,128)} %copy-done.1) | copy-start | bytes 786436
  80.8 8.8 %copy-start.4 = (f32[256,256]{1,0:T(8,128)S(1)}, f32[256,256]{1,0:T(8,128)}, u32[]{:S(2)}) copy-start(f32[256,256]{1,0:T(8,128)} %copy-done.3) | copy-start | bytes 786436
  81.6 9.6 %collective-permute-start.2 = (f32[3,320,128]{2,1,0:T(8,128)}, f32[3,320,128]{2,1,0:T(8,128)S(1)}, u32[]{:S(2)}, u32[]{:S(2)}) collective-permute-start(f32[3,320,128]{2,1,0:T(8,128)} %get-tuple-element.73), channel_id=1, source_target_pairs={{0,8},{8,16},{16,24},{24,32},{32,40},{40,48},{48,56},{56,64},{64,7... | collective-permute-start | bytes 1474568 | tf_op jit(solution)/shard_map/ppermute | solution.py:18
  88.2 7.5 %collective-permute-start.3 = (f32[3,320,128]{2,1,0:T(8,128)S(1)}, f32[3,320,128]{2,1,0:T(8,128)}, u32[]{:S(2)}, u32[]{:S(2)}) collective-permute-start(f32[3,320,128]{2,1,0:T(8,128)S(1)} %get-tuple-element.74), channel_id=1, source_target_pairs={{8,0},{16,8},{24,16},{32,24},{40,32},{48,40},{56,48},{64,56},{72,6... | collective-permute-start | bytes 1474568 | tf_op jit(solution)/shard_map/ppermute | solution.py:19
  91.2 269.9 %reduce-scatter.2.cloned.1.call-start = ((), (), s32[]{:S(2)}) async-start(), calls=%async_computation.1 | async-start | bytes 552960 | tf_op jit(solution)/shard_map/reduce_scatter | solution.py:131
  97.6 264.2 %copy-start.5 = (f32[2,40,128]{2,1,0:T(8,128)S(1)}, f32[2,40,128]{2,1,0:T(8,128)}, u32[]{:S(2)}) copy-start(f32[2,40,128]{2,1,0:T(8,128)} %param.14) | copy-start | bytes 122884
Sparse Core Ops, SparseCore 0:
  91.3 264.5 all-reduce.2
Sparse Core Ops, SparseCore 1:
  97.8 51.0 reduce-scatter.1
where the time goes:
time: 371 us
  waiting for transfers between devices  262 us (71%)
  blocking collectives  29.8 us (8%)
  matrix products  24.1 us (6%)
  between operations  19 us (5%)
  starting transfers between devices  12.3 us (3%)
  local copies, waits for them, and re-layouts  11.9 us (3%)
  other arithmetic  11.4 us (3%)
    psum x1, waiting for transfers between devices, local(): lax.psum((probe_grad, window_light), ('tile', 'group'))  258 us
    all_gather x1, blocking collectives, local(): full_rows = lax.all_gather(object_field, 'group', axis=1, tiled=True)  29.8 us
    dot_general x8, matrix products, apply_right(): jnp.einsum('pjk,kl->pjl', values, matrix, precision=lax.Precision.HIGHEST)  12.3 us
    dot_general x8, matrix products, apply_left(): jnp.einsum('jk,pkl->pjl', matrix, values, precision=lax.Precision.HIGHEST)  11.8 us
    dynamic_update_slice x1, local copies, waits for them, and re-layouts, place(): return lax.dynamic_update_slice(current, piece + terms[slot], corner)  10.9 us
    ppermute x2, starting transfers between devices, padded_2(): before = lax.ppermute(last, axis, up)  9.64 us
  transfers between devices with their start and end apart: 6, of which 2 were waited for; matrix products, arithmetic and copies ran while one was open for 2% of the time, Pallas kernels for 0%

commit v1 on v0

--- a/solution.py
+++ b/solution.py
@@ -129,7 +129,7 @@
     arrived = padded_2(edge_strips(accum), (("tile", 2),), HALO)
     summed = add_edges(accum[:, :, HALO : accum.shape[2] - HALO], arrived)
     share = lax.psum_scatter(summed, "group", scatter_dimension=1, tiled=True)
-    probe_grad, window_light = lax.psum((probe_grad, window_light), ("tile", "group"))
+    probe_grad, window_light = lax.psum(lax.psum((probe_grad, window_light), "tile"), "group")
     object_field, probe_field = apply_updates(
         object_field, probe_field, share, probe_grad, window_light
     )

time: 371 us -> 446 us (1.20)
  waiting for transfers between devices: 262 us -> 336 us
    psum x1 -> x2, waiting for transfers between devices: 258 us -> 330 us  [the longest x1 252 us: local(): lax.psum((probe_grad, window_light), 'tile')]
  transfers between devices with their start and end apart: 6 -> 7, of which waited for: 2 -> 4; matrix products, arithmetic and copies ran while one was open for 2% -> 3% of each run, Pallas kernels for 0% -> 0%
where the time goes in v1:
time: 446 us; the launch traced here: 443 us
  waiting for transfers between devices  336 us (75%)
  blocking collectives  29.8 us (7%)
  matrix products  24.1 us (5%)
  between operations  19 us (4%)
  starting transfers between devices  12.4 us (3%)
  local copies, waits for them, and re-layouts  11.1 us (2%)
  other arithmetic  10.4 us (2%)
    psum x1, waiting for transfers between devices, local(): lax.psum((probe_grad, window_light), 'tile')  252 us
    psum x1, waiting for transfers between devices, local(): lax.psum(lax.psum((probe_grad, window_light), 'tile'), 'group')  78.2 us
    all_gather x1, blocking collectives, local(): full_rows = lax.all_gather(object_field, 'group', axis=1, tiled=True)  29.8 us
    dot_general x8, matrix products, apply_right(): jnp.einsum('pjk,kl->pjl', values, matrix, precision=lax.Precision.HIGHEST)  12.3 us
    dot_general x8, matrix products, apply_left(): jnp.einsum('jk,pkl->pjl', matrix, values, precision=lax.Precision.HIGHEST)  11.8 us
    dynamic_update_slice x1, local copies, waits for them, and re-layouts, place(): return lax.dynamic_update_slice(current, piece + terms[slot], corner)  10.9 us
    ppermute x2, starting transfers between devices, padded_2(): before = lax.ppermute(last, axis, up)  9.66 us
  transfers between devices with their start and end apart: 7, of which 4 were waited for; matrix products, arithmetic and copies ran while one was open for 3% of the time, Pallas kernels for 0%

profile of v1, /device:TPU:2, one launch (start us, length us, event | category | flops | bytes accessed | tf_op | source)
XLA Modules:
  0.0 443.0 jit_solution(8342381134769947265)
XLA Ops:
  8.1 29.8 %all_gather.3 = f32[2,320,128]{2,1,0:T(8,128)S(1)} all-gather(f32[2,40,128]{2,1,0:T(8,128)} %param.14), channel_id=1, replica_groups=mesh['tile'=32,'group'=8] {'group'}, dimensions={1}, use_global_device_ids=true | all-gather | bytes 368640 | tf_op jit(solution)/shard_map/all_gather | solution.py:121
  39.2 3.1 collective-permute-start
  44.7 1.5 fusion.38
  47.7 1.5 fusion.9
  49.2 1.5 fusion.7
  50.6 1.5 fusion.47
  52.1 1.5 fusion.48
  53.6 1.5 fusion.4
  55.1 1.7 bitcast_multiply_fusion.11
  56.9 1.5 fusion.31
  58.4 1.5 fusion.27
  59.8 1.5 fusion.3
  61.3 1.5 fusion.2
  62.8 1.5 fusion.45
  64.3 1.5 fusion.46
  65.8 1.5 fusion
  67.3 1.7 fusion.1
  71.6 10.9 %dynamic_update_slice.4 = f32[3,320,384]{2,1,0:T(8,128)S(1)} dynamic-update-slice(f32[3,320,384]{2,1,0:T(8,128)S(1)} %broadcast_in_dim.6, f32[3,256,256]{2,1,0:T(8,128)S(1)} %maximum_bitcast_fusion, s32[]{:T(128)} %constant.112.clone.1, s32[]{:T(128)S(6)} %select_n.60, s32[]{:T(128)S(6)} %select_n.61) | dynamic-update-slice | bytes 1572868 | tf_op jit(solution)/shard_map/while/body/eval_jaxpr/dynamic_update_slice | solution.py:86
  82.6 6.6 %collective-permute-start.2 = (f32[3,320,128]{2,1,0:T(8,128)S(1)}, f32[3,320,128]{2,1,0:T(8,128)S(1)}, u32[]{:S(2)}, u32[]{:S(2)}) collective-permute-start(f32[3,320,128]{2,1,0:T(8,128)S(1)} %get-tuple-element.75), channel_id=1, source_target_pairs={{0,8},{8,16},{16,24},{24,32},{32,40},{40,48},{48,56},{56,64},{64,7... | collective-permute-start | bytes 1474568 | tf_op jit(solution)/shard_map/ppermute | solution.py:18
  90.6 5.9 %collective-permute-done.3 = f32[3,320,128]{2,1,0:T(8,128)S(1)} collective-permute-done((f32[3,320,128]{2,1,0:T(8,128)S(1)}, f32[3,320,128]{2,1,0:T(8,128)S(1)}, u32[]{:S(2)}, u32[]{:S(2)}) %collective-permute-start.3) | collective-permute-done | bytes 491552 | tf_op jit(solution)/shard_map/ppermute | solution.py:19
  97.5 251.9 %all-reduce.5.cloned.1.call-done = (f32[2,256,256]{2,1,0:T(8,128)}, f32[256,256]{1,0:T(8,128)}) async-done(((f32[2,256,256]{2,1,0:T(8,128)}, f32[256,256]{1,0:T(8,128)}), (f32[2,256,256]{2,1,0:T(8,128)}, f32[256,256]{1,0:T(8,128)})) %all-reduce.5.cloned.1.call-update) | async-done | bytes 786448 | tf_op jit(solution)/shard_map/psum | solution.py:132
  352.2 78.2 %all-reduce.7.cloned.1.call-done = (f32[2,256,256]{2,1,0:T(8,128)}, f32[256,256]{1,0:T(8,128)}) async-done(((f32[2,256,256]{2,1,0:T(8,128)}, f32[256,256]{1,0:T(8,128)}), (f32[2,256,256]{2,1,0:T(8,128)}, f32[256,256]{1,0:T(8,128)})) %all-reduce.7.cloned.1.call-update) | async-done | bytes 786448 | tf_op jit(solution)/shard_map/psum | solution.py:132
  430.4 1.6 reduce_sum.8
  433.6 1.9 divide_subtract_fusion
  (31 shorter events, 11.4 us)
Async XLA Ops:
  8.0 36.6 %copy-start = (f32[2,256,256]{2,1,0:T(8,128)S(1)}, f32[2,256,256]{2,1,0:T(8,128)}, u32[]{:S(2)}) copy-start(f32[2,256,256]{2,1,0:T(8,128)} %param.15) | copy-start | bytes 1572868
  8.0 341.4 %all-reduce.5.cloned.1.call-start = ((), (), s32[]{:S(2)}) async-start(), calls=%async_computation.2 | async-start | bytes 1572864 | tf_op jit(solution)/shard_map/psum | solution.py:132
  37.9 6.3 %collective-permute-start.1 = (f32[2,320,128]{2,1,0:T(8,128)S(1)}, f32[2,320,128]{2,1,0:T(8,128)S(1)}, u32[]{:S(2)}, u32[]{:S(2)}) collective-permute-start(f32[2,320,128]{2,1,0:T(8,128)S(1)} %all_gather.3), channel_id=1, source_target_pairs={{8,0},{16,8},{24,16},{32,24},{40,32},{48,40},{56,48},{64,56},{72,6... | collective-permute-start | bytes 983048 | tf_op jit(solution)/shard_map/ppermute | solution.py:19
  39.2 5.0 %collective-permute-start = (f32[2,320,128]{2,1,0:T(8,128)S(1)}, f32[2,320,128]{2,1,0:T(8,128)S(1)}, u32[]{:S(2)}, u32[]{:S(2)}) collective-permute-start(f32[2,320,128]{2,1,0:T(8,128)S(1)} %all_gather.3), channel_id=1, source_target_pairs={{0,8},{8,16},{16,24},{24,32},{32,40},{40,48},{48,56},{56,64},{64,7... | collective-permute-start | bytes 983048 | tf_op jit(solution)/shard_map/ppermute | solution.py:18
  52.1 3.0 copy-start.2
  71.3 278.7 %reduce-scatter.2.cloned.1.call-start = ((), (), s32[]{:S(2)}) async-start(), calls=%async_computation.1 | async-start | bytes 552960 | tf_op jit(solution)/shard_map/reduce_scatter | solution.py:131
  82.6 8.1 %collective-permute-start.2 = (f32[3,320,128]{2,1,0:T(8,128)S(1)}, f32[3,320,128]{2,1,0:T(8,128)S(1)}, u32[]{:S(2)}, u32[]{:S(2)}) collective-permute-start(f32[3,320,128]{2,1,0:T(8,128)S(1)} %get-tuple-element.75), channel_id=1, source_target_pairs={{0,8},{8,16},{16,24},{24,32},{32,40},{40,48},{48,56},{56,64},{64,7... | collective-permute-start | bytes 1474568 | tf_op jit(solution)/shard_map/ppermute | solution.py:18
  89.2 261.6 %copy-start.1 = (f32[2,40,128]{2,1,0:T(8,128)S(1)}, f32[2,40,128]{2,1,0:T(8,128)}, u32[]{:S(2)}) copy-start(f32[2,40,128]{2,1,0:T(8,128)} %param.14) | copy-start | bytes 122884
  89.2 7.4 %collective-permute-start.3 = (f32[3,320,128]{2,1,0:T(8,128)S(1)}, f32[3,320,128]{2,1,0:T(8,128)S(1)}, u32[]{:S(2)}, u32[]{:S(2)}) collective-permute-start(f32[3,320,128]{2,1,0:T(8,128)S(1)} %get-tuple-element.76), channel_id=1, source_target_pairs={{8,0},{16,8},{24,16},{32,24},{40,32},{48,40},{56,48},{64,56},{72,6... | collective-permute-start | bytes 1474568 | tf_op jit(solution)/shard_map/ppermute | solution.py:19
  97.5 332.9 %all-reduce.7.cloned.1.call-start = ((), (), s32[]{:S(2)}) async-start(), calls=%async_computation.3 | async-start | bytes 1572864 | tf_op jit(solution)/shard_map/psum | solution.py:132
Sparse Core Ops, SparseCore 0:
  71.5 277.8 all-reduce.4
Sparse Core Ops, SparseCore 1:
  97.5 51.7 reduce-scatter.1
  349.5 80.8 all-reduce.6
